TPU v7x, 128 devices: a whole 4x4x4 slice. The times are simulated.
128 devices in a mesh: row: 16 (over x, z), col: 8 (over y, core).
Axes of the slice: x: 4, y: 4, z: 4, core: 2. Of those that a mesh axis runs over, the one named last changes fastest.
Arguments:
- teacher_rows: bfloat16 [256, 8192], P('col', 'row'), may hold values from -6 to 6
- projection: bfloat16 [8192, 4608], P('row'), may hold values from -0.0625 to 0.0625
- student_in: bfloat16 [256, 4608], P('col', 'row'), may hold values from -36 to 36, as said below
- norm_gain: bfloat16 [4608], P('row'), may hold values from 0.5 to 1.5
- w_gate: bfloat16 [4608, 36864], P('row', 'col'), may hold values from -0.09375 to 0.09375
- w_up: bfloat16 [4608, 36864], P('row', 'col'), may hold values from -0.09375 to 0.09375
- w_down: bfloat16 [4608, 36864], P('row', 'col'), may hold values from -0.03125 to 0.03125
- row_old: float32 [3, 4608], P(None, 'row'), may hold values from 1.953125e-05 to 0.001953125
- col_old: float32 [3, 36864], P(None, 'col'), may hold values from 1.953125e-05 to 0.001953125
Outputs:
- update_gate: bfloat16 [4608, 36864], P('row', 'col')
- update_up: bfloat16 [4608, 36864], P('row', 'col')
- update_down: bfloat16 [4608, 36864], P('row', 'col')
- row_factors: float32 [3, 4608], P(None, 'row')
- col_factors: float32 [3, 36864], P(None, 'col')
- distill_loss: float32 [], replicated
Inputs may be any that keep to these rules, and one draw needn't show every extreme that they name: `student_in`: student hidden rows of varying magnitude.
All inputs are finite; a program needn't handle non-finite values.
Results may differ from a plain program's by a relative error of at most 0.0075.
Values may be sent and summed in bfloat16 or wider, within the bound.
A program may use at most 128 MiB of HBM per device.

v0:
```python
import math
import jax
import jax.numpy as jnp
from jax import lax
from jax.sharding import PartitionSpec as P

D = 4608
FF = 36864


def gelu_pair(values):
    root_coef = math.sqrt(2.0 / math.pi)
    tangent = jnp.tanh(root_coef * (values + 0.044715 * values * values * values))
    gelu_val = 0.5 * values * (1.0 + tangent)
    gelu_slope = 0.5 * (1.0 + tangent) + 0.5 * values * (1.0 - tangent * tangent) * root_coef * (
        1.0 + 3.0 * 0.044715 * values * values
    )
    return (gelu_val, gelu_slope)


def shards(teacher_rows, projection, student_in, norm_gain, w_gate, w_up, w_down, row_old, col_old):
    decay_rate = 0.8
    target = lax.psum_scatter(
        lax.dot_general(
            projection, teacher_rows, (((0,), (1,)), ((), ())), preferred_element_type=jnp.float32
        ),
        "row",
        scatter_dimension=0,
        tiled=True,
    ).T.astype(jnp.bfloat16)
    inputs = student_in.astype(jnp.float32)
    mean_sq = lax.psum(jnp.sum(inputs * inputs, axis=1), "row") / D
    inv_rms = (1.0 / jnp.sqrt(mean_sq + 1e-06))[:, None]
    normed = (inputs * inv_rms * norm_gain.astype(jnp.float32)[None, :]).astype(jnp.bfloat16)
    normed_all = lax.all_gather(normed, "col", axis=0, tiled=True)
    tokens_all = normed_all.shape[0]
    gate_part = jnp.dot(normed_all, w_gate, preferred_element_type=jnp.float32)
    up_part = jnp.dot(normed_all, w_up, preferred_element_type=jnp.float32)
    gate_sum, up_sum = lax.psum((gate_part, up_part), "row")
    gelu_val, gelu_slope = gelu_pair(gate_sum)
    hidden = (gelu_val * up_sum).astype(jnp.bfloat16)
    down_out = lax.psum_scatter(
        lax.dot_general(
            hidden, w_down, (((1,), (1,)), ((), ())), preferred_element_type=jnp.float32
        ),
        "col",
        scatter_dimension=0,
        tiled=True,
    )
    residue = inputs + down_out - target.astype(jnp.float32)
    loss_local = jnp.sum(residue * residue)
    loss_raw = lax.psum(loss_local, ("row", "col"))
    grad_out = (residue / tokens_all).astype(jnp.bfloat16)
    grad_all = lax.all_gather(grad_out, "col", axis=0, tiled=True)
    grad_down = lax.dot_general(
        grad_all, hidden, (((0,), (0,)), ((), ())), preferred_element_type=jnp.float32
    )
    hidden_part = jnp.dot(grad_all, w_down, preferred_element_type=jnp.float32)
    grad_hidden = lax.psum(hidden_part, "row")
    grad_gatein = (grad_hidden * up_sum * gelu_slope).astype(jnp.bfloat16)
    grad_upin = (grad_hidden * gelu_val).astype(jnp.bfloat16)
    grad_gate = lax.dot_general(
        normed_all, grad_gatein, (((0,), (0,)), ((), ())), preferred_element_type=jnp.float32
    )
    grad_up = lax.dot_general(
        normed_all, grad_upin, (((0,), (0,)), ((), ())), preferred_element_type=jnp.float32
    )
    gradients = [grad_gate, grad_up, grad_down]
    squares = [gradient * gradient + 1e-30 for gradient in gradients]
    row_sums = lax.psum(
        (jnp.sum(squares[0], axis=1), jnp.sum(squares[1], axis=1), jnp.sum(squares[2], axis=1)),
        "col",
    )
    col_sums = lax.psum(
        (jnp.sum(squares[0], axis=0), jnp.sum(squares[1], axis=0), jnp.sum(squares[2], axis=0)),
        "row",
    )
    row_new = [
        decay_rate * row_old[which] + (1.0 - decay_rate) * row_sums[which] / FF
        for which in range(3)
    ]
    col_new = [
        decay_rate * col_old[which] + (1.0 - decay_rate) * col_sums[which] / D for which in range(3)
    ]
    updates = [
        gradients[which] / jnp.sqrt(row_new[which][:, None] * col_new[which][None, :])
        for which in range(3)
    ]
    update_sums = [jnp.sum(update * update) for update in updates]
    totals = lax.psum((update_sums[0], update_sums[1], update_sums[2]), ("row", "col"))
    clipped = [
        (updates[which] / jnp.maximum(1.0, jnp.sqrt(totals[which] / (D * FF)))).astype(jnp.bfloat16)
        for which in range(3)
    ]
    loss_total = 0.5 * loss_raw / tokens_all
    return (clipped[0], clipped[1], clipped[2], jnp.stack(row_new), jnp.stack(col_new), loss_total)


def solution(mesh):
    placed = (
        P("col", "row"),
        P("row", None),
        P("col", "row"),
        P("row"),
        P("row", "col"),
        P("row", "col"),
        P("row", "col"),
        P(None, "row"),
        P(None, "col"),
    )
    return jax.shard_map(
        shards,
        mesh=mesh,
        in_specs=placed,
        out_specs=(
            P("row", "col"),
            P("row", "col"),
            P("row", "col"),
            P(None, "row"),
            P(None, "col"),
            P(),
        ),
        check_vma=False,
    )
```

profile of v0, /device:TPU:1, one launch (start us, length us, event | category | flops | bytes accessed | tf_op | source)
XLA Modules:
  0.0 661.3 jit_solution(16342523229148362279)
XLA Ops:
  8.9 35.4 %psum.98 = f32[32]{0:T(128)S(1)} all-reduce(f32[32]{0:T(128)S(1)} %fusion.16), channel_id=1, replica_groups=mesh['row'=16,'col'=8] {'row'}, use_global_device_ids=true, to_apply=%region_1.0 | all-reduce | flops 32 | bytes 256 | tf_op jit(solution)/shard_map/psum | solution.py:32
  45.3 20.9 %all_gather.6 = bf16[256,288]{1,0:T(8,128)(2,1)S(1)} all-gather(bf16[32,288]{1,0:T(8,128)(2,1)S(1)} %fusion.18), channel_id=1, replica_groups=mesh['row'=16,'col'=8] {'col'}, dimensions={0}, use_global_device_ids=true | all-gather | bytes 165888 | tf_op jit(solution)/shard_map/all_gather | solution.py:35
  66.2 5.3 fusion.29
  71.5 3.6 fusion.30
  75.8 5.7 fusion.33
  81.6 138.9 %all-reduce.9.cloned.1.call-done = (f32[256,4608]{1,0:T(8,128)}, f32[256,4608]{1,0:T(8,128)}) async-done(((f32[256,4608]{1,0:T(8,128)}, f32[256,4608]{1,0:T(8,128)}), (f32[256,4608]{1,0:T(8,128)}, f32[256,4608]{1,0:T(8,128)})) %all-reduce.9.cloned.1.call-update) | async-done | bytes 9437200 | tf_op jit(solution)/shard_map/psum | solution.py:39
  220.5 4.6 multiply_convert_fusion.1
  228.7 69.7 %reduce-scatter.7.cloned.1.call-done = f32[288,32]{1,0:T(8,128)} async-done(((f32[4608,32]{1,0:T(8,128)}), f32[288,32]{1,0:T(8,128)}) %reduce-scatter.7.cloned.1.call-update) | async-done | bytes 36880
  299.4 31.4 %reduce-scatter.5.cloned.1.call-done = f32[32,288]{1,0:T(8,128)} async-done(((f32[256,288]{1,0:T(8,128)}), f32[32,288]{1,0:T(8,128)}) %reduce-scatter.5.cloned.1.call-update) | async-done | bytes 36880 | tf_op jit(solution)/shard_map/reduce_scatter | solution.py:42
  332.3 16.1 %all_gather.7 = bf16[256,288]{1,0:T(8,128)(2,1)S(1)} all-gather(bf16[32,288]{1,0:T(8,128)(2,1)S(1)} %get-tuple-element.31), channel_id=1, replica_groups=mesh['row'=16,'col'=8] {'col'}, dimensions={0}, use_global_device_ids=true | all-gather | bytes 165888 | tf_op jit(solution)/shard_map/all_gather | solution.py:54
  348.3 3.6 fusion.32
  353.6 3.3 fusion.12
  356.9 102.5 %all-reduce.7.cloned.1.call-done = f32[256,4608]{1,0:T(8,128)} async-done(((f32[256,4608]{1,0:T(8,128)}), f32[256,4608]{1,0:T(8,128)}) %all-reduce.7.cloned.1.call-update) | async-done | bytes 4718608 | tf_op jit(solution)/shard_map/psum | solution.py:59
  459.3 9.0 %fusion.8 = (f32[288]{0:T(512)S(1)}, f32[4608]{0:T(1024)S(1)}, f32[288,4608]{1,0:T(8,128)}) fusion(bf16[256,288]{1,0:T(8,128)(2,1)S(1)} %all_gather.6, f32[256,4608]{1,0:T(8,128)} %get-tuple-element.25, f32[256,4608]{1,0:T(8,128)} %all-reduce.7.cloned.1.call-done, f32[256,4608]{1,0:T(8,128)} %get-tuple-element.26), kind=kOutput, calls=%fused_computation.24 | convolution fusion | flops 708373760 | bytes 19631232 | tf_op jit(solution)/shard_map/dot_general | solution.py:62
  468.3 7.3 %fusion.10 = (f32[288]{0:T(512)S(1)}, f32[4608]{0:T(1024)S(1)}, f32[288,4608]{1,0:T(8,128)}) fusion(bf16[256,288]{1,0:T(8,128)(2,1)S(1)} %all_gather.6, f32[256,4608]{1,0:T(8,128)S(1)} %copy-done.11, f32[256,4608]{1,0:T(8,128)} %get-tuple-element.25), kind=kOutput, calls=%fused_computation.26 | convolution fusion | flops 696577280 | bytes 14912640 | tf_op jit(solution)/shard_map/dot_general | solution.py:65
  475.7 12.8 %all-reduce.3 = (f32[288]{0:T(512)S(1)}, f32[288]{0:T(512)S(1)}, f32[288]{0:T(512)S(1)}) all-reduce(f32[288]{0:T(512)S(1)} %get-tuple-element.10, f32[288]{0:T(512)S(1)} %get-tuple-element.8, f32[288]{0:T(512)S(1)} %get-tuple-element.6), channel_id=1, replica_groups=mesh['row'=16,'col'=8] {'col'}, use_global_device_ids=true, to_apply=%region_8.0 | all-reduce | flops 864 | bytes 6912 | tf_op jit(solution)/shard_map/psum | solution.py:70
  488.5 58.5 %all-reduce.1 = (f32[4608]{0:T(1024)S(1)}, f32[4608]{0:T(1024)S(1)}, f32[4608]{0:T(1024)S(1)}) all-reduce(f32[4608]{0:T(1024)S(1)} %get-tuple-element.11, f32[4608]{0:T(1024)S(1)} %get-tuple-element.9, f32[4608]{0:T(1024)S(1)} %get-tuple-element.7), channel_id=1, replica_groups=mesh['row'=16,'col'=8] {'row'}, use_global_device_ids=true, to_apply=%region_10.0 | all-reduce | flops 13824 | bytes 110592 | tf_op jit(solution)/shard_map/psum | solution.py:74
  547.0 4.7 multiply_reduce_fusion.2
  551.7 2.4 multiply_reduce_fusion.1
  554.1 2.4 multiply_reduce_fusion
  556.5 78.3 %all-reduce = (f32[]{:T(128)}, f32[]{:T(128)}, f32[]{:T(128)}, f32[]{:T(128)}) all-reduce(f32[]{:T(128)} %multiply_reduce_fusion.2, f32[]{:T(128)} %multiply_reduce_fusion.1, f32[]{:T(128)} %multiply_reduce_fusion, f32[]{:T(128)} %get-tuple-element.30), channel_id=1, replica_groups=mesh['row'=16,'col'=8] {'row','col'}, use_global_device_ids=true, to_apply=%region_12.0 | all-reduce | flops 4 | bytes 32 | tf_op jit(solution)/shard_map/psum | solution.py:90
  635.5 4.9 divide_convert_fusion.2
  641.1 5.0 divide_convert_fusion.1
  646.8 4.9 divide_convert_fusion
  (53 shorter events, 12.5 us)
Async XLA Ops:
  7.2 219.3 %copy-start = (bf16[288,4608]{1,0:T(8,128)(2,1)S(1)}, bf16[288,4608]{1,0:T(8,128)(2,1)}, u32[]{:S(2)}) copy-start(bf16[288,4608]{1,0:T(8,128)(2,1)} %param.15) | copy-start | bytes 7962628
  7.2 213.3 %all-reduce.9.cloned.1.call-start = ((), (), s32[]{:S(2)}) async-start(), calls=%async_computation.5 | async-start | bytes 18874368 | tf_op jit(solution)/shard_map/psum | solution.py:39
  44.3 27.2 %copy-start.6 = (bf16[288,4608]{1,0:T(8,128)(2,1)S(1)}, bf16[288,4608]{1,0:T(8,128)(2,1)}, u32[]{:S(2)}) copy-start(bf16[288,4608]{1,0:T(8,128)(2,1)} %param.14) | copy-start | bytes 7962628
  75.0 0.8 copy-start.9
  75.1 223.4 %reduce-scatter.7.cloned.1.call-start = ((), (), s32[]{:S(2)}) async-start(), calls=%async_computation.4 | async-start | bytes 2506752
  81.5 249.3 %reduce-scatter.5.cloned.1.call-start = ((), (), s32[]{:S(2)}) async-start(), calls=%async_computation.2 | async-start | bytes 442368 | tf_op jit(solution)/shard_map/reduce_scatter | solution.py:42
  225.1 1.4 copy-start.4
  226.5 104.3 %copy-start.7 = (bf16[32,288]{1,0:T(8,128)(2,1)S(1)}, bf16[32,288]{1,0:T(8,128)(2,1)}, u32[]{:S(2)}) copy-start(bf16[32,288]{1,0:T(8,128)(2,1)} %param.11) | copy-start | bytes 55300
  228.7 230.7 %all-reduce.7.cloned.1.call-start = ((), (), s32[]{:S(2)}) async-start(), calls=%async_computation.3 | async-start | bytes 9437184 | tf_op jit(solution)/shard_map/psum | solution.py:59
  348.3 3.6 copy-start.10
  348.3 3.6 copy-start.8
  351.9 1.7 copy-start.5
  459.3 9.0 %copy-start.11 = (f32[256,4608]{1,0:T(8,128)S(1)}, f32[256,4608]{1,0:T(8,128)}, u32[]{:S(2)}) copy-start(f32[256,4608]{1,0:T(8,128)} %all-reduce.7.cloned.1.call-done) | copy-start | bytes 14155780
  546.9 4.8 copy-start.3
  547.0 7.2 %copy-start.2 = (f32[288,4608]{1,0:T(8,128)S(1)}, f32[288,4608]{1,0:T(8,128)}, u32[]{:S(2)}) copy-start(f32[288,4608]{1,0:T(8,128)} %get-tuple-element.34) | copy-start | bytes 15925252
  641.1 12.6 %copy-start.1 = (bf16[288,4608]{1,0:T(8,128)(2,1)S(1)}, bf16[288,4608]{1,0:T(8,128)(2,1)}, u32[]{:S(2)}) copy-start(bf16[288,4608]{1,0:T(8,128)(2,1)} %param.15) | copy-start | bytes 7962628
Sparse Core Ops, SparseCore 0:
  75.2 145.2 all-reduce.8
  224.4 74.0 reduce-scatter.6
  301.4 29.4 reduce-scatter.4
  352.1 107.2 all-reduce.6
where the time goes:
time: 662 us; the launch traced here: 661 us
  waiting for transfers between devices  343 us (52%)
  blocking collectives  222 us (34%)
  matrix products  39.8 us (6%)
  other arithmetic  34.5 us (5%)
  between operations  17.8 us (3%)
    psum x1, waiting for transfers between devices, shards(): gate_sum, up_sum = lax.psum((gate_part, up_part), 'row')  139 us
    psum x1, waiting for transfers between devices, shards(): grad_hidden = lax.psum(hidden_part, 'row')  102 us
    psum x1, blocking collectives, shards(): lax.psum((update_sums[0], update_sums[1], update_sums[2]), ('row', 'col'))  78.3 us
    unnamed x5, waiting for transfers between devices  69.8 us
    psum x1, blocking collectives, shards(): lax.psum((jnp.sum(squares[0], axis=0), jnp.sum(squares[1], axis=0), jnp.s...  58.5 us
    psum x1, blocking collectives, shards(): mean_sq = lax.psum(jnp.sum(inputs * inputs, axis=1), 'row') / D  35.4 us
    reduce_scatter x1, waiting for transfers between devices, shards(): lax.psum_scatter(lax.dot_general(hidden, w_down, (((1,), (1,)), ((), ()))...  31.4 us
    all_gather x1, blocking collectives, shards(): normed_all = lax.all_gather(normed, 'col', axis=0, tiled=True)  20.9 us
  transfers between devices with their start and end apart: 4, of which 4 were waited for; matrix products, arithmetic and copies ran while one was open for 3% of the time, Pallas kernels for 0%

commit v1 on v0

--- a/solution.py
+++ b/solution.py
@@ -56,7 +56,24 @@
         grad_all, hidden, (((0,), (0,)), ((), ())), preferred_element_type=jnp.float32
     )
     hidden_part = jnp.dot(grad_all, w_down, preferred_element_type=jnp.float32)
-    grad_hidden = lax.psum(hidden_part, "row")
+
+    def array_edit(x_part):
+        world_n = lax.axis_size("row")
+
+        def plan_stocks_here(state_now, piece_out):
+            if piece_out >= world_n:
+                return state_now
+            return plan_stocks_here(
+                state_now
+                + lax.ppermute(
+                    state_now, "row", list(map(lambda no: (no, no ^ piece_out), range(world_n)))
+                ),
+                2 * piece_out,
+            )
+
+        return plan_stocks_here(x_part, 1)
+
+    grad_hidden = array_edit(hidden_part)
     grad_gatein = (grad_hidden * up_sum * gelu_slope).astype(jnp.bfloat16)
     grad_upin = (grad_hidden * gelu_val).astype(jnp.bfloat16)
     grad_gate = lax.dot_general(

time: 662 us -> 962 us (1.45)
  waiting for transfers between devices: 343 us -> 639 us
    ppermute x0 -> x4, waiting for transfers between devices: none -> 399 us  [plan_stocks_here(): lax.ppermute(state_now, 'row', list(map(lambda no: (no, no ^ piece_out),...]
    psum x1 -> x0, waiting for transfers between devices: 102 us -> none  [shards(): grad_hidden = lax.psum(hidden_part, 'row')]
    unnamed x5 -> x4, waiting for transfers between devices: 69.8 us -> 69.8 us
  transfers between devices with their start and end apart: 4 -> 7, of which waited for: 4 -> 7; matrix products, arithmetic and copies ran while one was open for 3% -> 2% of each run, Pallas kernels for 0% -> 0%
where the time goes in v1:
time: 962 us; the launch traced here: 961 us
  waiting for transfers between devices  639 us (66%)
  blocking collectives  225 us (23%)
  other arithmetic  36.1 us (4%)
  matrix products  31.5 us (3%)
  between operations  17.8 us (2%)
    ppermute x4, waiting for transfers between devices, plan_stocks_here(): lax.ppermute(state_now, 'row', list(map(lambda no: (no, no ^ piece_out),...  399 us
    psum x1, waiting for transfers between devices, shards(): gate_sum, up_sum = lax.psum((gate_part, up_part), 'row')  139 us
    psum x1, blocking collectives, shards(): lax.psum((update_sums[0], update_sums[1], update_sums[2]), ('row', 'col'))  76.6 us
    unnamed x4, waiting for transfers between devices  69.8 us
    psum x1, blocking collectives, shards(): lax.psum((jnp.sum(squares[0], axis=0), jnp.sum(squares[1], axis=0), jnp.s...  60.4 us
    psum x1, blocking collectives, shards(): mean_sq = lax.psum(jnp.sum(inputs * inputs, axis=1), 'row') / D  35.4 us
    reduce_scatter x1, waiting for transfers between devices, shards(): lax.psum_scatter(lax.dot_general(hidden, w_down, (((1,), (1,)), ((), ()))...  31.4 us
    all_gather x1, blocking collectives, shards(): normed_all = lax.all_gather(normed, 'col', axis=0, tiled=True)  20.9 us
  transfers between devices with their start and end apart: 7, of which 7 were waited for; matrix products, arithmetic and copies ran while one was open for 2% of the time, Pallas kernels for 0%

profile of v1, /device:TPU:1, one launch (start us, length us, event | category | flops | bytes accessed | tf_op | source)
XLA Modules:
  0.0 961.3 jit_solution(4182792174013705139)
XLA Ops:
  8.9 35.4 %psum.91 = f32[32]{0:T(128)S(1)} all-reduce(f32[32]{0:T(128)S(1)} %fusion.18), channel_id=1, replica_groups=mesh['row'=16,'col'=8] {'row'}, use_global_device_ids=true, to_apply=%region_1.0 | all-reduce | flops 32 | bytes 256 | tf_op jit(solution)/shard_map/psum | solution.py:32
  45.3 20.9 %all_gather.6 = bf16[256,288]{1,0:T(8,128)(2,1)S(1)} all-gather(bf16[32,288]{1,0:T(8,128)(2,1)S(1)} %fusion.20), channel_id=1, replica_groups=mesh['row'=16,'col'=8] {'col'}, dimensions={0}, use_global_device_ids=true | all-gather | bytes 165888 | tf_op jit(solution)/shard_map/all_gather | solution.py:35
  66.2 5.3 fusion.31
  71.5 3.5 fusion.32
  75.8 5.7 fusion.35
  81.5 138.9 %all-reduce.6.cloned.1.call-done = (f32[256,4608]{1,0:T(8,128)}, f32[256,4608]{1,0:T(8,128)}) async-done(((f32[256,4608]{1,0:T(8,128)}, f32[256,4608]{1,0:T(8,128)}), (f32[256,4608]{1,0:T(8,128)}, f32[256,4608]{1,0:T(8,128)})) %all-reduce.6.cloned.1.call-update) | async-done | bytes 9437200 | tf_op jit(solution)/shard_map/psum | solution.py:39
  220.5 4.6 multiply_convert_fusion.1
  228.6 69.8 %reduce-scatter.7.cloned.1.call-done = f32[288,32]{1,0:T(8,128)} async-done(((f32[4608,32]{1,0:T(8,128)}), f32[288,32]{1,0:T(8,128)}) %reduce-scatter.7.cloned.1.call-update) | async-done | bytes 36880
  299.4 31.4 %reduce-scatter.5.cloned.1.call-done = f32[32,288]{1,0:T(8,128)} async-done(((f32[256,288]{1,0:T(8,128)}), f32[32,288]{1,0:T(8,128)}) %reduce-scatter.5.cloned.1.call-update) | async-done | bytes 36880 | tf_op jit(solution)/shard_map/reduce_scatter | solution.py:42
  332.2 15.9 %all_gather.7 = bf16[256,288]{1,0:T(8,128)(2,1)S(1)} all-gather(bf16[32,288]{1,0:T(8,128)(2,1)S(1)} %get-tuple-element.31), channel_id=1, replica_groups=mesh['row'=16,'col'=8] {'col'}, dimensions={0}, use_global_device_ids=true | all-gather | bytes 165888 | tf_op jit(solution)/shard_map/all_gather | solution.py:54
  350.8 102.0 %collective-permute-done = f32[256,4608]{1,0:T(8,128)S(1)} collective-permute-done((f32[256,4608]{1,0:T(8,128)S(1)}, f32[256,4608]{1,0:T(8,128)S(1)}, u32[]{:S(2)}, u32[]{:S(2)}) %collective-permute-start) | collective-permute-done | bytes 4718624 | tf_op jit(solution)/shard_map/ppermute | solution.py:68
  456.3 101.0 %collective-permute-done.1 = f32[256,4608]{1,0:T(8,128)S(1)} collective-permute-done((f32[256,4608]{1,0:T(8,128)S(1)}, f32[256,4608]{1,0:T(8,128)S(1)}, u32[]{:S(2)}, u32[]{:S(2)}) %collective-permute-start.1) | collective-permute-done | bytes 4718624 | tf_op jit(solution)/shard_map/ppermute | solution.py:68
  559.1 100.3 %collective-permute-done.2 = f32[256,4608]{1,0:T(8,128)S(1)} collective-permute-done((f32[256,4608]{1,0:T(8,128)S(1)}, f32[256,4608]{1,0:T(8,128)S(1)}, u32[]{:S(2)}, u32[]{:S(2)}) %collective-permute-start.2) | collective-permute-done | bytes 4718624 | tf_op jit(solution)/shard_map/ppermute | solution.py:68
  663.0 3.3 fusion.12
  666.3 96.0 %collective-permute-done.3 = f32[256,4608]{1,0:T(8,128)S(1)} collective-permute-done((f32[256,4608]{1,0:T(8,128)S(1)}, f32[256,4608]{1,0:T(8,128)S(1)}, u32[]{:S(2)}, u32[]{:S(2)}) %collective-permute-start.3) | collective-permute-done | bytes 4718624 | tf_op jit(solution)/shard_map/ppermute | solution.py:68
  762.4 5.7 fusion.8
  768.1 4.4 fusion.10
  772.6 15.5 %all-reduce.3 = (f32[288]{0:T(512)S(1)}, f32[288]{0:T(512)S(1)}, f32[288]{0:T(512)S(1)}) all-reduce(f32[288]{0:T(512)S(1)} %get-tuple-element.10, f32[288]{0:T(512)S(1)} %get-tuple-element.8, f32[288]{0:T(512)S(1)} %get-tuple-element.6), channel_id=1, replica_groups=mesh['row'=16,'col'=8] {'col'}, use_global_device_ids=true, to_apply=%region_7.0 | all-reduce | flops 864 | bytes 6912 | tf_op jit(solution)/shard_map/psum | solution.py:87
  788.1 60.4 %all-reduce.1 = (f32[4608]{0:T(1024)S(1)}, f32[4608]{0:T(1024)S(1)}, f32[4608]{0:T(1024)S(1)}) all-reduce(f32[4608]{0:T(1024)S(1)} %get-tuple-element.11, f32[4608]{0:T(1024)S(1)} %get-tuple-element.9, f32[4608]{0:T(1024)S(1)} %get-tuple-element.7), channel_id=1, replica_groups=mesh['row'=16,'col'=8] {'row'}, use_global_device_ids=true, to_apply=%region_9.0 | all-reduce | flops 13824 | bytes 110592 | tf_op jit(solution)/shard_map/psum | solution.py:91
  848.5 4.7 multiply_reduce_fusion.2
  858.1 76.6 %all-reduce = (f32[]{:T(128)}, f32[]{:T(128)}, f32[]{:T(128)}, f32[]{:T(128)}) all-reduce(f32[]{:T(128)} %multiply_reduce_fusion.2, f32[]{:T(128)} %multiply_reduce_fusion.1, f32[]{:T(128)} %multiply_reduce_fusion, f32[]{:T(128)} %get-tuple-element.30), channel_id=1, replica_groups=mesh['row'=16,'col'=8] {'row','col'}, use_global_device_ids=true, to_apply=%region_11.0 | all-reduce | flops 4 | bytes 32 | tf_op jit(solution)/shard_map/psum | solution.py:107
  935.4 4.9 divide_convert_fusion.2
  941.0 5.0 divide_convert_fusion.1
  946.8 4.9 divide_convert_fusion
  (69 shorter events, 27.2 us)
Async XLA Ops:
  7.2 219.3 %copy-start = (bf16[288,4608]{1,0:T(8,128)(2,1)S(1)}, bf16[288,4608]{1,0:T(8,128)(2,1)}, u32[]{:S(2)}) copy-start(bf16[288,4608]{1,0:T(8,128)(2,1)} %param.15) | copy-start | bytes 7962628
  7.2 213.3 %all-reduce.6.cloned.1.call-start = ((), (), s32[]{:S(2)}) async-start(), calls=%async_computation.4 | async-start | bytes 18874368 | tf_op jit(solution)/shard_map/psum | solution.py:39
  44.3 27.2 %copy-start.6 = (bf16[288,4608]{1,0:T(8,128)(2,1)S(1)}, bf16[288,4608]{1,0:T(8,128)(2,1)}, u32[]{:S(2)}) copy-start(bf16[288,4608]{1,0:T(8,128)(2,1)} %param.14) | copy-start | bytes 7962628
  75.0 0.8 copy-start.9
  75.0 223.4 %reduce-scatter.7.cloned.1.call-start = ((), (), s32[]{:S(2)}) async-start(), calls=%async_computation.3 | async-start | bytes 2506752
  81.5 249.3 %reduce-scatter.5.cloned.1.call-start = ((), (), s32[]{:S(2)}) async-start(), calls=%async_computation.2 | async-start | bytes 442368 | tf_op jit(solution)/shard_map/reduce_scatter | solution.py:42
  225.1 1.4 copy-start.4
  226.5 104.3 %copy-start.7 = (bf16[32,288]{1,0:T(8,128)(2,1)S(1)}, bf16[32,288]{1,0:T(8,128)(2,1)}, u32[]{:S(2)}) copy-start(bf16[32,288]{1,0:T(8,128)(2,1)} %param.11) | copy-start | bytes 55300
  349.5 103.3 %collective-permute-start = (f32[256,4608]{1,0:T(8,128)S(1)}, f32[256,4608]{1,0:T(8,128)S(1)}, u32[]{:S(2)}, u32[]{:S(2)}) collective-permute-start(f32[256,4608]{1,0:T(8,128)S(1)} %fusion.34), channel_id=1, source_target_pairs={{0,8},{8,0},{16,24},{24,16},{32,40},{40,32},{48,56},{56,48},{64,72... | collective-permute-start | bytes 14155784 | tf_op jit(solution)/shard_map/ppermute | solution.py:68
  453.3 103.9 %collective-permute-start.1 = (f32[256,4608]{1,0:T(8,128)S(1)}, f32[256,4608]{1,0:T(8,128)S(1)}, u32[]{:S(2)}, u32[]{:S(2)}) collective-permute-start(f32[256,4608]{1,0:T(8,128)S(1)} %add.96), channel_id=1, source_target_pairs={{0,16},{8,24},{16,0},{24,8},{32,48},{40,56},{48,32},{56,40},{64,80... | collective-permute-start | bytes 14155784 | tf_op jit(solution)/shard_map/ppermute | solution.py:68
  557.3 205.1 %slice-start = ((s8[4718592]{0:T(1024)(128)(4,1)}), s8[4194304]{0:T(1024)(128)(4,1)S(1)}, s32[]{:S(2)}) async-start(s8[4718592]{0:T(1024)(128)(4,1)} %bitcast.21), calls=%async_computation.5 | async-start | bytes 8388608
  557.3 205.1 %slice-start.2 = ((s8[4718592]{0:T(1024)(128)(4,1)}), s8[4194304]{0:T(1024)(128)(4,1)S(1)}, s32[]{:S(2)}) async-start(s8[4718592]{0:T(1024)(128)(4,1)} %bitcast.23), calls=%async_computation.7 | async-start | bytes 8388608
  557.8 105.0 %copy-start.10 = (f32[3,288]{1,0:T(4,128)S(1)}, f32[3,288]{1,0:T(4,128)}, u32[]{:S(2)}) copy-start(f32[3,288]{1,0:T(4,128)} %param.16) | copy-start | bytes 10372
  557.8 105.0 %copy-start.8 = (f32[3,4608]{1,0:T(4,128)S(1)}, f32[3,4608]{1,0:T(4,128)}, u32[]{:S(2)}) copy-start(f32[3,4608]{1,0:T(4,128)} %param.17) | copy-start | bytes 165892
  557.8 105.2 %copy-start.5 = (bf16[256,4608]{1,0:T(8,128)(2,1)S(1)}, bf16[256,4608]{1,0:T(8,128)(2,1)}, u32[]{:S(2)}) copy-start(bf16[256,4608]{1,0:T(8,128)(2,1)} %copy-done.4) | copy-start | bytes 7077892
  557.8 204.5 %slice-start.1 = ((s8[4718592]{0:T(1024)(128)(4,1)}), s8[524288]{0:T(1024)(128)(4,1)S(1)}, s32[]{:S(2)}) async-start(s8[4718592]{0:T(1024)(128)(4,1)} %bitcast.21), calls=%async_computation.6 | async-start | bytes 1048576
  557.8 204.5 %slice-start.3 = ((s8[4718592]{0:T(1024)(128)(4,1)}), s8[524288]{0:T(1024)(128)(4,1)S(1)}, s32[]{:S(2)}) async-start(s8[4718592]{0:T(1024)(128)(4,1)} %bitcast.23), calls=%async_computation.8 | async-start | bytes 1048576
  557.9 101.6 %collective-permute-start.2 = (f32[256,4608]{1,0:T(8,128)S(1)}, f32[256,4608]{1,0:T(8,128)S(1)}, u32[]{:S(2)}, u32[]{:S(2)}) collective-permute-start(f32[256,4608]{1,0:T(8,128)S(1)} %add.97), channel_id=1, source_target_pairs={{0,32},{8,40},{16,48},{24,56},{32,0},{40,8},{48,16},{56,24},{64,96... | collective-permute-start | bytes 14155784 | tf_op jit(solution)/shard_map/ppermute | solution.py:68
  660.0 102.4 %collective-permute-start.3 = (f32[256,4608]{1,0:T(8,128)S(1)}, f32[256,4608]{1,0:T(8,128)S(1)}, u32[]{:S(2)}, u32[]{:S(2)}) collective-permute-start(f32[256,4608]{1,0:T(8,128)S(1)} %add.98), channel_id=1, source_target_pairs={{0,64},{8,72},{16,80},{24,88},{32,96},{40,104},{48,112},{56,120},{... | collective-permute-start | bytes 14155784 | tf_op jit(solution)/shard_map/ppermute | solution.py:68
  848.5 4.8 copy-start.3
  848.5 7.2 copy-start.2
  941.0 12.6 %copy-start.1 = (bf16[288,4608]{1,0:T(8,128)(2,1)S(1)}, bf16[288,4608]{1,0:T(8,128)(2,1)}, u32[]{:S(2)}) copy-start(bf16[288,4608]{1,0:T(8,128)(2,1)} %param.15) | copy-start | bytes 7962628
Sparse Core Ops, SparseCore 0:
  75.2 145.2 all-reduce.5
  224.3 74.0 reduce-scatter.6
  301.3 29.4 reduce-scatter.4
